TPU v7x, 32 devices: a whole 2x2x4 slice. The times are simulated.
32 devices in a mesh: layer: 2 (over x), gx: 4 (over z), gy: 4 (over y, core).
Axes of the slice: x: 2, y: 2, z: 4, core: 2. Of those that a mesh axis runs over, the one named last changes fastest.
Arguments:
- pressure: float32 [16, 256, 1024], P('layer', 'gx', 'gy'), may hold values from -6 to 6
- source: float32 [16, 256, 1024], P('layer', 'gx', 'gy'), may hold values from -6 to 6
- perm_x: float32 [16, 256, 1024], P('layer', 'gx', 'gy'), may hold values from 0.05 to 0.5
- perm_y: float32 [16, 256, 1024], P('layer', 'gx', 'gy'), may hold values from 0.05 to 0.5
- line_inverse: float32 [2, 8, 8, 256, 1024], P('layer', None, None, 'gx', 'gy'), may hold values from -0.98 to 1.2
- robin_below: float32 [2, 256, 1024], P('layer', 'gx', 'gy'), may hold values from -6 to 6
- tile_count: int32 [2, 16], P('layer', ('gx', 'gy')), may hold values from 1 to 48, 256 in all within a row
- perf_owner: int32 [2, 768, 1], P('layer', ('gx', 'gy')), may hold values from 0 to 15; in each aligned block of 48 rows (0 to 47, 48 to 95, ..., all dimensions but the last counted through in order) at most 3 rows name the same one
- perf_well: int32 [2, 768], P('layer', ('gx', 'gy')), may hold values from 0 to 7
- perf_column: int32 [2, 768], P('layer', ('gx', 'gy')), may hold values from 0 to 16383
- perf_index: float32 [2, 768, 8], P('layer', ('gx', 'gy')), may hold values from 0.2 to 2
- well_rate: float32 [2, 128], P('layer', ('gx', 'gy')), may hold values from -8 to 8
Outputs:
- pressure_out: float32 [16, 256, 1024], P('layer', 'gx', 'gy')
- perf_flow: float32 [2, 768, 8], P('layer', ('gx', 'gy'))
Inputs may be any that keep to these rules, and one draw needn't show every extreme that they name: `tile_count`: live slots of a tile are its first ones; some tile of every group has all 48 live. `perf_owner`: among the 48 slots of one tile at most 3 name one owner.
All inputs are finite; a program needn't handle non-finite values.
Results may differ from a plain program's by a relative error of at most 0.00018.
Values sent between devices are 32-bit elements; how exact they have to be, the bound alone decides.
A program may use at most 64 MiB of HBM per device.

v0:
```python
import jax
import jax.numpy as jnp
from jax import lax
from jax.sharding import PartitionSpec as P

ITERS = 2


HIGHEST_PRECISION = lax.Precision.HIGHEST


def extended(value, sides, width):
    for axis, dim in sides:
        size, length = (lax.axis_size(axis), value.shape[dim])
        up = [(i, (i + 1) % size) for i in range(size - 1)]
        down = [(j, i) for i, j in up]
        last = lax.slice_in_dim(value, length - width, length, axis=dim)
        initial = lax.slice_in_dim(value, 0, width, axis=dim)
        before = lax.ppermute(last, axis, up)
        after = lax.ppermute(initial, axis, down)
        value = jnp.concatenate([before, value, after], axis=dim)
    return value


def passed_along(value, axis, steps):
    count = lax.axis_size(axis)
    initial, last = (max(0, -steps), min(count, count - steps))
    return lax.ppermute(value, axis, [(source, source + steps) for source in range(initial, last)])


def neighbours(padded_field, rock_x, rock_y, perm_x, perm_y):
    east_term = 0.5 * (perm_x + rock_x[:, 2:, 1:-1]) * padded_field[:, 2:, 1:-1]
    west_term = 0.5 * (perm_x + rock_x[:, :-2, 1:-1]) * padded_field[:, :-2, 1:-1]
    north_term = 0.5 * (perm_y + rock_y[:, 1:-1, 2:]) * padded_field[:, 1:-1, 2:]
    south_term = 0.5 * (perm_y + rock_y[:, 1:-1, :-2]) * padded_field[:, 1:-1, :-2]
    return east_term + west_term + (north_term + south_term)


def shards(
    pressure,
    source,
    perm_x,
    perm_y,
    line_inverse,
    robin_below,
    tile_count,
    perf_owner,
    perf_well,
    perf_column,
    perf_index,
    well_rate,
):
    layer_depth, width_x, width_y = pressure.shape
    columns = width_x * width_y
    tile_total = lax.axis_size(("gx", "gy"))
    slot_total = perf_well.shape[1]
    wells_own = well_rate.shape[1]
    capacity = max(2, (slot_total + tile_total - 1) // tile_total)
    rock_pair = jnp.stack([perm_x, perm_y])
    padded_rock = extended(rock_pair, (("gx", 2), ("gy", 3)), 1)
    rock_x = padded_rock[0]
    rock_y = padded_rock[1]
    inverse = line_inverse[0]
    live_slot = jnp.arange(slot_total) < tile_count[0, 0]
    owner_of = perf_owner[0, :, 0]
    owner_hits = (
        (owner_of[:, None] == jnp.arange(tile_total)[None, :]) & live_slot[:, None]
    ).astype(jnp.int32)
    earlier = (jnp.arange(slot_total)[None, :] < jnp.arange(slot_total)[:, None]).astype(jnp.int32)
    before = jnp.dot(earlier, owner_hits)
    slot_rank = jnp.sum(before * owner_hits, axis=1)
    target = owner_of * capacity + slot_rank
    placing = (jnp.arange(tile_total * capacity)[:, None] == target[None, :]) & live_slot[None, :]
    place_float = placing.astype(jnp.float32)
    slot_ids = jnp.sum(placing.astype(jnp.int32) * (perf_well[0] + 1)[None, :], axis=1).reshape(
        tile_total, capacity
    )
    ids_in = lax.all_to_all(
        slot_ids, ("gx", "gy"), split_axis=0, concat_axis=0, tiled=True
    ).reshape(tile_total * capacity)
    member = (ids_in[None, :] == jnp.arange(wells_own)[:, None] + 1).astype(jnp.float32)
    filled = (ids_in > 0).astype(jnp.float32)
    column = perf_column[0]
    index_slots = perf_index[0]
    field_now = pressure
    lower_data = robin_below[0]
    slot_flow = jnp.zeros((slot_total, layer_depth), jnp.float32)
    a_down = inverse[layer_depth - 1, 0]
    g_last = inverse[layer_depth - 1, layer_depth - 1]
    g_first = inverse[0, 0]
    a_up = inverse[0, layer_depth - 1]
    for sweep_step in range(ITERS):
        padded_field = extended(field_now, (("gx", 1), ("gy", 2)), 1)
        lateral = neighbours(padded_field, rock_x, rock_y, perm_x, perm_y)
        flat_field = field_now.reshape(layer_depth, columns)
        at_slots = jnp.take(flat_field, column, axis=1).T
        stacked = jnp.concatenate([at_slots, index_slots], axis=1)
        outgoing = jnp.dot(place_float, stacked, precision=HIGHEST_PRECISION).reshape(
            tile_total, capacity, 2 * layer_depth
        )
        both_in = lax.all_to_all(
            outgoing, ("gx", "gy"), split_axis=0, concat_axis=0, tiled=True
        ).reshape(tile_total * capacity, 2 * layer_depth)
        received = both_in[:, :layer_depth]
        index_here = both_in[:, layer_depth:]
        index_sum = jnp.dot(member, jnp.sum(index_here, axis=1), precision=HIGHEST_PRECISION)
        weighted_sum = jnp.dot(
            member, jnp.sum(index_here * received, axis=1), precision=HIGHEST_PRECISION
        )
        bottom_hole = (well_rate[0] + weighted_sum) / (index_sum + 1.0)
        hole_slots = jnp.dot(bottom_hole, member, precision=HIGHEST_PRECISION)
        flow_out = index_here * (hole_slots[:, None] - received) * filled[:, None]
        returned = lax.all_to_all(
            flow_out.reshape(tile_total, capacity, layer_depth),
            ("gx", "gy"),
            split_axis=0,
            concat_axis=0,
            tiled=True,
        ).reshape(tile_total * capacity, layer_depth)
        well_slot_flow = jnp.dot(place_float.T, returned, precision=HIGHEST_PRECISION)
        well_term = (
            jnp.zeros((layer_depth, columns), jnp.float32)
            .at[:, column]
            .add(well_slot_flow.T)
            .reshape(layer_depth, width_x, width_y)
        )
        well_term, slot_flow = (well_term, well_slot_flow)
        rhs = source + lateral + well_term
        solved = jnp.einsum("ijxy,jxy->ixy", inverse, rhs, precision=HIGHEST_PRECISION)
        c_down = solved[layer_depth - 1] + g_last * lower_data - lower_data
        upper_trace = jnp.zeros_like(lower_data)
        for link_step in range(lax.axis_size("layer") - 1):
            upper_trace = passed_along(a_down * upper_trace + c_down, "layer", 1)
        c_up = solved[0] + g_first * upper_trace - upper_trace
        lower_trace = jnp.zeros_like(lower_data)
        for link_step in range(lax.axis_size("layer") - 1):
            lower_trace = passed_along(a_up * lower_trace + c_up, "layer", -1)
        lower_data = lower_trace
        field_now = (
            solved
            + inverse[:, 0] * upper_trace[None]
            + inverse[:, layer_depth - 1] * lower_trace[None]
        )
    return (field_now, slot_flow[None])


def solution(mesh):
    placed = (
        P("layer", "gx", "gy"),
        P("layer", "gx", "gy"),
        P("layer", "gx", "gy"),
        P("layer", "gx", "gy"),
        P("layer", None, None, "gx", "gy"),
        P("layer", "gx", "gy"),
        P("layer", ("gx", "gy")),
        P("layer", ("gx", "gy"), None),
        P("layer", ("gx", "gy")),
        P("layer", ("gx", "gy")),
        P("layer", ("gx", "gy"), None),
        P("layer", ("gx", "gy")),
    )
    return jax.shard_map(
        shards,
        mesh=mesh,
        in_specs=placed,
        out_specs=(P("layer", "gx", "gy"), P("layer", ("gx", "gy"), None)),
        check_vma=False,
    )
```

profile of v0, /device:TPU:0, one launch (start us, length us, event | category | flops | bytes accessed | tf_op | source)
XLA Modules:
  0.0 160.4 jit_solution(4213163899798468288)
XLA Ops:
  4.4 7.4 %all-to-all-start.1 = ((s32[16,1,3]{2,1,0:T(1,128)}), s32[16,1,3]{2,1,0:T(1,128)S(1)}, u32[]{:S(2)}, u32[]{:S(2)}) async-start(s32[16,1,3]{2,1,0:T(1,128)} %bitcast.19), calls=%async_computation.1 | async-start | bytes 16384 | tf_op jit(solution)/shard_map/all_to_all | solution.py:78
  13.2 3.8 %collective-permute-start.5 = (f32[8,1,256]{2,0,1:T(8,128)S(1)}, f32[8,1,256]{2,0,1:T(8,128)S(1)}, u32[]{:S(2)}, u32[]{:S(2)}) collective-permute-start(f32[8,1,256]{2,0,1:T(8,128)S(1)} %get-tuple-element.28), channel_id=1, source_target_pairs={{0,4},{4,8},{8,12},{1,5},{5,9},{9,13},{2,6},{6,10},{10,14},{3,7},{... | collective-permute-start | bytes 24584 | tf_op jit(solution)/shard_map/ppermute | solution.py:19
  18.3 1.8 %copy_bitcast_fusion.1 = (f32[1,8,64,256]{3,1,2,0:T(8,128)S(1)}, f32[1,8,64,256]{3,1,2,0:T(8,128)S(1)}) fusion(f32[8,64,256]{2,1,0:T(8,128)} %param.16, f32[8,64,256]{2,1,0:T(8,128)} %param.17), kind=kLoop, calls=%fused_computation.82 | loop fusion | bytes 2097152 | tf_op jit(solution)/shard_map/stack | solution.py:59
  21.5 5.3 %collective-permute-start = (f32[2,8,1,256]{3,1,2,0:T(8,128)S(1)}, f32[2,8,1,256]{3,1,2,0:T(8,128)S(1)}, u32[]{:S(2)}, u32[]{:S(2)}) collective-permute-start(f32[2,8,1,256]{3,1,2,0:T(8,128)S(1)} %get-tuple-element.19), channel_id=1, source_target_pairs={{0,4},{4,8},{8,12},{1,5},{5,9},{9,13},{2,6},{6,10},{10,14},{3,7},{... | collective-permute-start | bytes 49160 | tf_op jit(solution)/shard_map/ppermute | solution.py:19
  26.8 4.6 %copy.110 = f32[8,64,256]{0,2,1:T(8,128)} copy(f32[8,64,256]{2,1,0:T(8,128)S(1)} %copy-done.2) | data formatting | bytes 1048576 | tf_op args[0]
  31.5 4.0 %gather_fusion = f32[48,8]{1,0:T(8,128)S(1)} fusion(f32[8,16384]{0,1:T(8,128)} %bitcast.192, s32[1024]{0:T(1024)S(1)} %pad_clamp_fusion), kind=kCustom, calls=%fused_computation.clone | custom fusion | bytes 3264 | tf_op jit(solution)/shard_map/jit(_take)/gather | solution.py:96
  36.4 5.2 %all-to-all-start = ((f32[16,3,16]{2,1,0:T(4,128)}), f32[16,3,16]{2,1,0:T(4,128)S(1)}, u32[]{:S(2)}, u32[]{:S(2)}) async-start(f32[16,3,16]{2,1,0:T(4,128)} %reshape.120), calls=%async_computation | async-start | bytes 65536 | tf_op jit(solution)/shard_map/all_to_all | solution.py:101
  42.9 5.3 %all-to-all-done = f32[16,3,16]{2,1,0:T(4,128)S(1)} async-done(((f32[16,3,16]{2,1,0:T(4,128)}), f32[16,3,16]{2,1,0:T(4,128)S(1)}, u32[]{:S(2)}, u32[]{:S(2)}) %all-to-all-start) | async-done | bytes 3104 | tf_op jit(solution)/shard_map/all_to_all | solution.py:101
  49.8 3.5 %all-to-all-start.2 = ((f32[16,3,8]{2,1,0:T(4,128)}), f32[16,3,8]{2,1,0:T(4,128)S(1)}, u32[]{:S(2)}, u32[]{:S(2)}) async-start(f32[16,3,8]{2,1,0:T(4,128)} %reshape.122), calls=%async_computation.2 | async-start | bytes 65536 | tf_op jit(solution)/shard_map/all_to_all | solution.py:113
  54.5 2.2 %collective-permute-start.7 = (f32[8,66,1]{2,0,1:T(8,128)}, f32[8,66,1]{2,0,1:T(8,128)S(1)}, u32[]{:S(2)}, u32[]{:S(2)}) collective-permute-start(f32[8,66,1]{2,0,1:T(8,128)} %get-tuple-element.24), channel_id=1, source_target_pairs={{0,1},{1,2},{2,3},{4,5},{5,6},{6,7},{8,9},{9,10},{10,11},{12,13},{... | collective-permute-start | bytes 6344 | tf_op jit(solution)/shard_map/ppermute | solution.py:19
  58.0 1.8 %all-to-all-done.2 = f32[16,3,8]{2,1,0:T(4,128)S(1)} async-done(((f32[16,3,8]{2,1,0:T(4,128)}), f32[16,3,8]{2,1,0:T(4,128)S(1)}, u32[]{:S(2)}, u32[]{:S(2)}) %all-to-all-start.2) | async-done | bytes 1568 | tf_op jit(solution)/shard_map/all_to_all | solution.py:113
  62.1 3.0 %collective-permute-start.2 = (f32[2,8,66,1]{2,1,3,0:T(8,128)S(1)}, f32[2,8,66,1]{2,1,3,0:T(8,128)S(1)}, u32[]{:S(2)}, u32[]{:S(2)}) collective-permute-start(f32[2,8,66,1]{2,1,3,0:T(8,128)S(1)} %copy.96), channel_id=1, source_target_pairs={{0,1},{1,2},{2,3},{4,5},{5,6},{6,7},{8,9},{9,10},{10,11},{12,13},{... | collective-permute-start | bytes 12680 | tf_op jit(solution)/shard_map/ppermute | solution.py:19
  65.3 4.5 %scatter_custom_fusion = f32[8,16384]{0,1:T(8,128)} fusion(s32[48]{0:T(128)S(1)} %fusion.97, f32[48,8]{1,0:T(8,128)S(1)} %fusion.61, f32[]{:T(128)} %constant.16.clone.1), kind=kCustom, calls=%fused_computation.10 | custom fusion | flops 384 | bytes 524292 | tf_op jit(solution)/shard_map/scatter-add | solution.py:124
  69.9 5.9 %copy.115 = f32[8,64,256]{2,0,1:T(8,128)} copy(f32[8,64,256]{0,2,1:T(8,128)} %bitcast.186) | data formatting | bytes 1048576 | tf_op jit(solution)/shard_map/reshape | solution.py:125
  77.2 1.8 %pad_maximum_fusion = f32[2,8,66,258]{3,1,2,0:T(8,128)S(1)} fusion(f32[2,8,66,1]{3,1,2,0:T(8,128)S(1)} %copy.99, f32[2,8,1,256]{3,1,2,0:T(8,128)S(1)} %collective-permute-done.1, f32[1,8,64,256]{3,1,2,0:T(8,128)S(1)} %get-tuple-element.30, f32[1,8,64,256]{3,1,2,0:T(8,128)S(1)} %get-tuple-element.29, f32[2,8,1,256]{3,1,2,0:T(8,128)S(1)} %collective-permute-done, ...), kind=kLoop, calls=%fused_computation.12 | loop fusion | flops 1362240 | bytes 2179584 | tf_op jit(solution)/shard_map/concatenate | solution.py:21
  79.1 2.7 %fusion.30 = f32[64,256,8]{1,2,0:T(8,128)S(1)} fusion(f32[8,64,256]{2,0,1:T(8,128)S(1)} %copy-done.6, f32[8,66,256]{2,0,1:T(8,128)S(1)} %constant_dynamic-update-slice_fusion, f32[8,66,1]{2,0,1:T(8,128)S(1)} %collective-permute-done.7, f32[8,66,1]{2,0,1:T(8,128)} %collective-permute-done.6, f32[8,64,256]{2,0,1:T(8,128)} %copy-done.5, ...), kind=kLoop, calls=%fused_computation.57 | loop fusion | flops 2752512 | bytes 5804160
  82.7 3.4 %collective-permute-start.8 = (f32[64,256]{1,0:T(8,128)S(1)}, f32[64,256]{1,0:T(8,128)S(1)}, u32[]{:S(2)}, u32[]{:S(2)}) collective-permute-start(f32[64,256]{1,0:T(8,128)S(1)} %fusion.52), channel_id=1, source_target_pairs={{0,16},{1,17},{2,18},{3,19},{4,20},{5,21},{6,22},{7,23},{8,24},{9,... | collective-permute-start | bytes 196616 | tf_op jit(solution)/shard_map/ppermute | solution.py:28
  89.4 5.3 %collective-permute-done.9 = f32[64,256]{1,0:T(8,128)S(1)} collective-permute-done((f32[64,256]{1,0:T(8,128)S(1)}, f32[64,256]{1,0:T(8,128)S(1)}, u32[]{:S(2)}, u32[]{:S(2)}) %collective-permute-start.9) | collective-permute-done | bytes 65568 | tf_op jit(solution)/shard_map/ppermute | solution.py:28
  95.7 4.8 %copy.120 = f32[8,64,256]{0,2,1:T(8,128)} copy(f32[8,64,256]{2,0,1:T(8,128)S(1)} %fusion.39) | data formatting | bytes 1048576 | tf_op jit(solution)/shard_map/add | solution.py:140
  100.5 4.0 %gather_fusion.1 = f32[48,8]{1,0:T(8,128)S(1)} fusion(f32[8,16384]{0,1:T(8,128)} %bitcast.193, s32[1024]{0:T(1024)S(1)} %pad_clamp_fusion), kind=kCustom, calls=%fused_computation.1.clone | custom fusion | bytes 3264 | tf_op jit(solution)/shard_map/jit(_take)/gather | solution.py:96
  105.4 5.7 %all-to-all-start.3 = ((f32[16,3,16]{2,1,0:T(4,128)}), f32[16,3,16]{2,1,0:T(4,128)S(1)}, u32[]{:S(2)}, u32[]{:S(2)}) async-start(f32[16,3,16]{2,1,0:T(4,128)} %reshape.126), calls=%async_computation.3 | async-start | bytes 65536 | tf_op jit(solution)/shard_map/all_to_all | solution.py:101
  112.4 4.5 %collective-permute-start.11 = (f32[8,1,256]{2,0,1:T(8,128)S(1)}, f32[8,1,256]{2,0,1:T(8,128)S(1)}, u32[]{:S(2)}, u32[]{:S(2)}) collective-permute-start(f32[8,1,256]{2,0,1:T(8,128)S(1)} %get-tuple-element.25), channel_id=1, source_target_pairs={{0,4},{4,8},{8,12},{1,5},{5,9},{9,13},{2,6},{6,10},{10,14},{3,7},{... | collective-permute-start | bytes 24584 | tf_op jit(solution)/shard_map/ppermute | solution.py:19
  119.2 4.4 %all-to-all-start.4 = ((f32[16,3,8]{2,1,0:T(4,128)}), f32[16,3,8]{2,1,0:T(4,128)}, u32[]{:S(2)}, u32[]{:S(2)}) async-start(f32[16,3,8]{2,1,0:T(4,128)} %reshape.128), calls=%async_computation.4 | async-start | bytes 65536 | tf_op jit(solution)/shard_map/all_to_all | solution.py:113
  124.6 2.3 %collective-permute-start.13 = (f32[8,66,1]{2,0,1:T(8,128)}, f32[8,66,1]{2,0,1:T(8,128)S(1)}, u32[]{:S(2)}, u32[]{:S(2)}) collective-permute-start(f32[8,66,1]{2,0,1:T(8,128)} %get-tuple-element.22), channel_id=1, source_target_pairs={{0,1},{1,2},{2,3},{4,5},{5,6},{6,7},{8,9},{9,10},{10,11},{12,13},{... | collective-permute-start | bytes 6344 | tf_op jit(solution)/shard_map/ppermute | solution.py:19
  128.2 2.1 %all-to-all-done.4 = f32[16,3,8]{2,1,0:T(4,128)} async-done(((f32[16,3,8]{2,1,0:T(4,128)}), f32[16,3,8]{2,1,0:T(4,128)}, u32[]{:S(2)}, u32[]{:S(2)}) %all-to-all-start.4) | async-done | bytes 1568 | tf_op jit(solution)/shard_map/all_to_all | solution.py:113
  131.7 1.5 fusion.57
  134.6 4.7 %scatter_custom_fusion.1 = f32[8,16384]{0,1:T(8,128)} fusion(s32[48]{0:T(128)} %copy-done.19, f32[48,8]{1,0:T(8,128)} %copy.123, f32[]{:T(128)} %constant.16.clone.1), kind=kCustom, calls=%fused_computation.8 | custom fusion | flops 384 | bytes 524800 | tf_op jit(solution)/shard_map/scatter-add | solution.py:124
  139.3 5.9 %copy.124 = f32[8,64,256]{2,0,1:T(8,128)} copy(f32[8,64,256]{0,2,1:T(8,128)} %bitcast.185) | data formatting | bytes 1048576 | tf_op jit(solution)/shard_map/reshape | solution.py:125
  145.2 3.0 %fusion.20 = f32[64,256,8]{1,2,0:T(8,128)S(1)} fusion(f32[8,64,256]{2,0,1:T(8,128)} %copy.124, f32[8,66,1]{2,0,1:T(8,128)S(1)} %collective-permute-done.13, f32[8,1,256]{2,0,1:T(8,128)S(1)} %collective-permute-done.10, f32[8,64,256]{2,0,1:T(8,128)S(1)} %fusion.39, f32[8,1,256]{2,0,1:T(8,128)S(1)} %collective-permute-done.11, ...), kind=kLoop, calls=%fused_computation.39 | loop fusion | flops 3276800 | bytes 5263488
  149.0 1.6 collective-permute-start.14
  150.5 1.9 %collective-permute-done.14 = f32[64,256]{1,0:T(8,128)S(1)} collective-permute-done((f32[64,256]{1,0:T(8,128)S(1)}, f32[64,256]{1,0:T(8,128)S(1)}, u32[]{:S(2)}, u32[]{:S(2)}) %collective-permute-start.14) | collective-permute-done | bytes 65568 | tf_op jit(solution)/shard_map/ppermute | solution.py:28
  153.7 4.9 %collective-permute-done.15 = f32[64,256]{1,0:T(8,128)S(1)} collective-permute-done((f32[64,256]{1,0:T(8,128)S(1)}, f32[64,256]{1,0:T(8,128)S(1)}, u32[]{:S(2)}, u32[]{:S(2)}) %collective-permute-start.15) | collective-permute-done | bytes 65568 | tf_op jit(solution)/shard_map/ppermute | solution.py:28
  (139 shorter events, 35.5 us)
Async XLA Ops:
  0.6 26.2 %copy-start.2 = (f32[8,64,256]{2,1,0:T(8,128)S(1)}, f32[8,64,256]{2,1,0:T(8,128)}, u32[]{:S(2)}) copy-start(f32[8,64,256]{2,1,0:T(8,128)} %param.14) | copy-start | bytes 1572868
  4.4 32.0 %all-to-all-start.1 = ((s32[16,1,3]{2,1,0:T(1,128)}), s32[16,1,3]{2,1,0:T(1,128)S(1)}, u32[]{:S(2)}, u32[]{:S(2)}) async-start(s32[16,1,3]{2,1,0:T(1,128)} %bitcast.19), calls=%async_computation.1 | async-start | bytes 16384 | tf_op jit(solution)/shard_map/all_to_all | solution.py:78
  13.2 40.1 %collective-permute-start.5 = (f32[8,1,256]{2,0,1:T(8,128)S(1)}, f32[8,1,256]{2,0,1:T(8,128)S(1)}, u32[]{:S(2)}, u32[]{:S(2)}) collective-permute-start(f32[8,1,256]{2,0,1:T(8,128)S(1)} %get-tuple-element.28), channel_id=1, source_target_pairs={{0,4},{4,8},{8,12},{1,5},{5,9},{9,13},{2,6},{6,10},{10,14},{3,7},{... | collective-permute-start | bytes 24584 | tf_op jit(solution)/shard_map/ppermute | solution.py:19
  17.0 36.6 %collective-permute-start.4 = (f32[8,1,256]{2,0,1:T(8,128)S(1)}, f32[8,1,256]{2,0,1:T(8,128)S(1)}, u32[]{:S(2)}, u32[]{:S(2)}) collective-permute-start(f32[8,1,256]{2,0,1:T(8,128)S(1)} %get-tuple-element.27), channel_id=1, source_target_pairs={{4,0},{8,4},{12,8},{5,1},{9,5},{13,9},{6,2},{10,6},{14,10},{7,3},{... | collective-permute-start | bytes 24584 | tf_op jit(solution)/shard_map/ppermute | solution.py:20
  20.1 39.8 %collective-permute-start.1 = (f32[2,8,1,256]{3,1,2,0:T(8,128)S(1)}, f32[2,8,1,256]{3,1,2,0:T(8,128)S(1)}, u32[]{:S(2)}, u32[]{:S(2)}) collective-permute-start(f32[2,8,1,256]{3,1,2,0:T(8,128)S(1)} %get-tuple-element.20), channel_id=1, source_target_pairs={{4,0},{8,4},{12,8},{5,1},{9,5},{13,9},{6,2},{10,6},{14,10},{7,3},{... | collective-permute-start | bytes 49160 | tf_op jit(solution)/shard_map/ppermute | solution.py:20
  21.4 14.2 %copy-start.9 = (f32[1,48,8]{1,2,0:T(8,128)S(1)}, f32[1,48,8]{1,2,0:T(8,128)}, u32[]{:S(2)}) copy-start(f32[1,48,8]{1,2,0:T(8,128)} %param.24) | copy-start | bytes 4612
  21.5 27.2 %copy-start.17 = (f32[1,8]{1,0:T(1,128)S(1)}, f32[1,8]{1,0:T(1,128)}, u32[]{:S(2)}) copy-start(f32[1,8]{1,0:T(1,128)} %param.25) | copy-start | bytes 100
  21.5 38.4 %collective-permute-start = (f32[2,8,1,256]{3,1,2,0:T(8,128)S(1)}, f32[2,8,1,256]{3,1,2,0:T(8,128)S(1)}, u32[]{:S(2)}, u32[]{:S(2)}) collective-permute-start(f32[2,8,1,256]{3,1,2,0:T(8,128)S(1)} %get-tuple-element.19), channel_id=1, source_target_pairs={{0,4},{4,8},{8,12},{1,5},{5,9},{9,13},{2,6},{6,10},{10,14},{3,7},{... | collective-permute-start | bytes 49160 | tf_op jit(solution)/shard_map/ppermute | solution.py:19
  31.4 33.9 %copy-start.19 = (s32[48]{0:T(128)}, s32[48]{0:T(128)S(1)}, u32[]{:S(2)}) copy-start(s32[48]{0:T(128)S(1)} %fusion.97) | copy-start | bytes 580
  35.8 24.1 %copy-start.20 = (s32[8]{0:T(128)}, s32[8]{0:T(128)S(1)}, u32[]{:S(2)}) copy-start(s32[8]{0:T(128)S(1)} %iota_add_fusion) | copy-start | bytes 100
  36.4 11.8 %all-to-all-start = ((f32[16,3,16]{2,1,0:T(4,128)}), f32[16,3,16]{2,1,0:T(4,128)S(1)}, u32[]{:S(2)}, u32[]{:S(2)}) async-start(f32[16,3,16]{2,1,0:T(4,128)} %reshape.120), calls=%async_computation | async-start | bytes 65536 | tf_op jit(solution)/shard_map/all_to_all | solution.py:101
  42.9 17.0 %copy-start.14 = (s32[48]{0:T(128)}, s32[48]{0:T(128)S(1)}, u32[]{:S(2)}) copy-start(s32[48]{0:T(128)S(1)} %eq.50) | copy-start | bytes 580
  42.9 17.0 %copy-start.10 = (f32[48]{0:T(128)}, f32[48]{0:T(128)S(1)}, u32[]{:S(2)}) copy-start(f32[48]{0:T(128)S(1)} %compare_convert_fusion) | copy-start | bytes 580
  49.8 10.1 %all-to-all-start.2 = ((f32[16,3,8]{2,1,0:T(4,128)}), f32[16,3,8]{2,1,0:T(4,128)S(1)}, u32[]{:S(2)}, u32[]{:S(2)}) async-start(f32[16,3,8]{2,1,0:T(4,128)} %reshape.122), calls=%async_computation.2 | async-start | bytes 65536 | tf_op jit(solution)/shard_map/all_to_all | solution.py:113
  54.5 24.5 %collective-permute-start.7 = (f32[8,66,1]{2,0,1:T(8,128)}, f32[8,66,1]{2,0,1:T(8,128)S(1)}, u32[]{:S(2)}, u32[]{:S(2)}) collective-permute-start(f32[8,66,1]{2,0,1:T(8,128)} %get-tuple-element.24), channel_id=1, source_target_pairs={{0,1},{1,2},{2,3},{4,5},{5,6},{6,7},{8,9},{9,10},{10,11},{12,13},{... | collective-permute-start | bytes 6344 | tf_op jit(solution)/shard_map/ppermute | solution.py:19
  56.7 22.4 %collective-permute-start.6 = (f32[8,66,1]{2,0,1:T(8,128)}, f32[8,66,1]{2,0,1:T(8,128)}, u32[]{:S(2)}, u32[]{:S(2)}) collective-permute-start(f32[8,66,1]{2,0,1:T(8,128)} %get-tuple-element.23), channel_id=1, source_target_pairs={{1,0},{2,1},{3,2},{5,4},{6,5},{7,6},{9,8},{10,9},{11,10},{13,12},{... | collective-permute-start | bytes 6344 | tf_op jit(solution)/shard_map/ppermute | solution.py:20
  60.5 15.2 %collective-permute-start.3 = (f32[2,8,66,1]{2,1,3,0:T(8,128)S(1)}, f32[2,8,66,1]{2,1,3,0:T(8,128)S(1)}, u32[]{:S(2)}, u32[]{:S(2)}) collective-permute-start(f32[2,8,66,1]{2,1,3,0:T(8,128)S(1)} %copy.97), channel_id=1, source_target_pairs={{1,0},{2,1},{3,2},{5,4},{6,5},{7,6},{9,8},{10,9},{11,10},{13,12},{... | collective-permute-start | bytes 12680 | tf_op jit(solution)/shard_map/ppermute | solution.py:20
  62.1 14.0 %collective-permute-start.2 = (f32[2,8,66,1]{2,1,3,0:T(8,128)S(1)}, f32[2,8,66,1]{2,1,3,0:T(8,128)S(1)}, u32[]{:S(2)}, u32[]{:S(2)}) collective-permute-start(f32[2,8,66,1]{2,1,3,0:T(8,128)S(1)} %copy.96), channel_id=1, source_target_pairs={{0,1},{1,2},{2,3},{4,5},{5,6},{6,7},{8,9},{9,10},{10,11},{12,13},{... | collective-permute-start | bytes 12680 | tf_op jit(solution)/shard_map/ppermute | solution.py:19
  82.7 5.3 %collective-permute-start.8 = (f32[64,256]{1,0:T(8,128)S(1)}, f32[64,256]{1,0:T(8,128)S(1)}, u32[]{:S(2)}, u32[]{:S(2)}) collective-permute-start(f32[64,256]{1,0:T(8,128)S(1)} %fusion.52), channel_id=1, source_target_pairs={{0,16},{1,17},{2,18},{3,19},{4,20},{5,21},{6,22},{7,23},{8,24},{9,... | collective-permute-start | bytes 196616 | tf_op jit(solution)/shard_map/ppermute | solution.py:28
  88.0 6.7 %collective-permute-start.9 = (f32[64,256]{1,0:T(8,128)S(1)}, f32[64,256]{1,0:T(8,128)S(1)}, u32[]{:S(2)}, u32[]{:S(2)}) collective-permute-start(f32[64,256]{1,0:T(8,128)S(1)} %fusion.55), channel_id=1, source_target_pairs={{16,0},{17,1},{18,2},{19,3},{20,4},{21,5},{22,6},{23,7},{24,8},{25... | collective-permute-start | bytes 196616 | tf_op jit(solution)/shard_map/ppermute | solution.py:28
  95.6 22.3 %copy-start.15 = (s32[48]{0:T(128)S(1)}, s32[48]{0:T(128)}, u32[]{:S(2)}) copy-start(s32[48]{0:T(128)} %copy-done.14) | copy-start | bytes 580
  95.6 22.3 %copy-start.21 = (s32[8]{0:T(128)S(1)}, s32[8]{0:T(128)}, u32[]{:S(2)}) copy-start(s32[8]{0:T(128)} %copy-done.20) | copy-start | bytes 100
  95.6 22.5 %copy-start.18 = (f32[1,8]{1,0:T(1,128)S(1)}, f32[1,8]{1,0:T(1,128)}, u32[]{:S(2)}) copy-start(f32[1,8]{1,0:T(1,128)} %param.25) | copy-start | bytes 100
  95.6 22.8 %copy-start.11 = (f32[48]{0:T(128)S(1)}, f32[48]{0:T(128)}, u32[]{:S(2)}) copy-start(f32[48]{0:T(128)} %copy-done.10) | copy-start | bytes 580
  105.4 12.3 %all-to-all-start.3 = ((f32[16,3,16]{2,1,0:T(4,128)}), f32[16,3,16]{2,1,0:T(4,128)S(1)}, u32[]{:S(2)}, u32[]{:S(2)}) async-start(f32[16,3,16]{2,1,0:T(4,128)} %reshape.126), calls=%async_computation.3 | async-start | bytes 65536 | tf_op jit(solution)/shard_map/all_to_all | solution.py:101
  111.1 12.6 %collective-permute-start.10 = (f32[8,1,256]{2,0,1:T(8,128)S(1)}, f32[8,1,256]{2,0,1:T(8,128)S(1)}, u32[]{:S(2)}, u32[]{:S(2)}) collective-permute-start(f32[8,1,256]{2,0,1:T(8,128)S(1)} %get-tuple-element.26), channel_id=1, source_target_pairs={{4,0},{8,4},{12,8},{5,1},{9,5},{13,9},{6,2},{10,6},{14,10},{7,3},{... | collective-permute-start | bytes 24584 | tf_op jit(solution)/shard_map/ppermute | solution.py:20
  112.4 11.3 %collective-permute-start.11 = (f32[8,1,256]{2,0,1:T(8,128)S(1)}, f32[8,1,256]{2,0,1:T(8,128)S(1)}, u32[]{:S(2)}, u32[]{:S(2)}) collective-permute-start(f32[8,1,256]{2,0,1:T(8,128)S(1)} %get-tuple-element.25), channel_id=1, source_target_pairs={{0,4},{4,8},{8,12},{1,5},{5,9},{9,13},{2,6},{6,10},{10,14},{3,7},{... | collective-permute-start | bytes 24584 | tf_op jit(solution)/shard_map/ppermute | solution.py:19
  119.2 11.1 %all-to-all-start.4 = ((f32[16,3,8]{2,1,0:T(4,128)}), f32[16,3,8]{2,1,0:T(4,128)}, u32[]{:S(2)}, u32[]{:S(2)}) async-start(f32[16,3,8]{2,1,0:T(4,128)} %reshape.128), calls=%async_computation.4 | async-start | bytes 65536 | tf_op jit(solution)/shard_map/all_to_all | solution.py:113
  124.6 20.6 %collective-permute-start.13 = (f32[8,66,1]{2,0,1:T(8,128)}, f32[8,66,1]{2,0,1:T(8,128)S(1)}, u32[]{:S(2)}, u32[]{:S(2)}) collective-permute-start(f32[8,66,1]{2,0,1:T(8,128)} %get-tuple-element.22), channel_id=1, source_target_pairs={{0,1},{1,2},{2,3},{4,5},{5,6},{6,7},{8,9},{9,10},{10,11},{12,13},{... | collective-permute-start | bytes 6344 | tf_op jit(solution)/shard_map/ppermute | solution.py:19
  126.9 18.3 %collective-permute-start.12 = (f32[8,66,1]{2,0,1:T(8,128)}, f32[8,66,1]{2,0,1:T(8,128)}, u32[]{:S(2)}, u32[]{:S(2)}) collective-permute-start(f32[8,66,1]{2,0,1:T(8,128)} %get-tuple-element.21), channel_id=1, source_target_pairs={{1,0},{2,1},{3,2},{5,4},{6,5},{7,6},{9,8},{10,9},{11,10},{13,12},{... | collective-permute-start | bytes 6344 | tf_op jit(solution)/shard_map/ppermute | solution.py:20
  149.0 3.5 %collective-permute-start.14 = (f32[64,256]{1,0:T(8,128)S(1)}, f32[64,256]{1,0:T(8,128)S(1)}, u32[]{:S(2)}, u32[]{:S(2)}) collective-permute-start(f32[64,256]{1,0:T(8,128)S(1)} %fusion.48), channel_id=1, source_target_pairs={{0,16},{1,17},{2,18},{3,19},{4,20},{5,21},{6,22},{7,23},{8,24},{9,... | collective-permute-start | bytes 196616 | tf_op jit(solution)/shard_map/ppermute | solution.py:28
  152.4 6.2 %collective-permute-start.15 = (f32[64,256]{1,0:T(8,128)S(1)}, f32[64,256]{1,0:T(8,128)S(1)}, u32[]{:S(2)}, u32[]{:S(2)}) collective-permute-start(f32[64,256]{1,0:T(8,128)S(1)} %fusion.45), channel_id=1, source_target_pairs={{16,0},{17,1},{18,2},{19,3},{20,4},{21,5},{22,6},{23,7},{24,8},{25... | collective-permute-start | bytes 196616 | tf_op jit(solution)/shard_map/ppermute | solution.py:28
  (11 other events, 45.3 us)
where the time goes:
time: 162 us; the launch traced here: 160 us
  starting transfers between devices  62.7 us (39%)
  local copies, waits for them, and re-layouts  45.4 us (28%)
  waiting for transfers between devices  23.7 us (15%)
  other arithmetic  22.6 us (14%)
  matrix products  4.04 us (2%)
  between operations  2.1 us (1%)
    ppermute x6, starting transfers between devices, extended(): before = lax.ppermute(last, axis, up)  21.2 us
    ppermute x4, waiting for transfers between devices, passed_along(): lax.ppermute(value, axis, [(source, source + steps) for source in range(i...  13.6 us
    reshape x2, local copies, waits for them, and re-layouts, shards(): well_term = jnp.zeros((layer_depth, columns), jnp.float32).at[:, column]....  11.7 us
    all_to_all x2, starting transfers between devices, shards(): lax.all_to_all(outgoing, ('gx', 'gy'), split_axis=0, concat_axis=0, tiled...  10.9 us
    scatter-add x2, other arithmetic, shards(): well_term = jnp.zeros((layer_depth, columns), jnp.float32).at[:, column]....  9.24 us
    gather x2, local copies, waits for them, and re-layouts, shards(): at_slots = jnp.take(flat_field, column, axis=1).T  7.93 us
    all_to_all x2, starting transfers between devices, shards(): lax.all_to_all(flow_out.reshape(tile_total, capacity, layer_depth), ('gx'...  7.9 us
    unnamed x51, local copies, waits for them, and re-layouts  7.81 us
  transfers between devices with their start and end apart: 21, of which 8 were waited for; matrix products, arithmetic and copies ran while one was open for 31% of the time, Pallas kernels for 0%

commit v1 on v0

v1 whole, which is shorter than its diff:
```python
import functools

import jax
import jax.numpy as jnp
from jax import lax
from jax.experimental import pallas as pl
from jax.experimental.pallas import tpu as pltpu
from jax.sharding import PartitionSpec as P

ITERS = 2
MESH = pl.DeviceIdType.MESH
F32 = jnp.float32
BF16 = jnp.bfloat16
ROWS = 8


def pieces(value):
    high = value.astype(BF16)
    rest = value - high.astype(F32)
    middle = rest.astype(BF16)
    low = (rest - middle.astype(F32)).astype(BF16)
    return jnp.concatenate([high, middle, low], axis=0)


def as_column(row):
    n = row.shape[1]
    eye = lax.broadcasted_iota(jnp.int32, (n, n), 0) == lax.broadcasted_iota(jnp.int32, (n, n), 1)
    return jnp.sum(jnp.where(eye, jnp.broadcast_to(row, (n, n)), 0.0), axis=1, keepdims=True)


def kernel(
    dims,
    pressure,
    source,
    perm_x,
    perm_y,
    inverse,
    robin,
    count_in,
    owner_in,
    well_in,
    column_in,
    index_in,
    rate_in,
    field_out,
    flow_out,
    field,
    src,
    kx,
    ky,
    inv,
    lower,
    count_v,
    owner_v,
    well_v,
    column_v,
    index_v,
    rate_v,
    upper,
    rhs,
    solved,
    flow_v,
    halo_mult_x,
    halo_mult_y,
    well_send0,
    well_recv0,
    well_send1,
    well_recv1,
    row_send,
    row_recv,
    col_send,
    col_recv,
    coef_recv,
    down_send,
    down_recv,
    up_send,
    up_recv,
    load_sem,
    store_sem,
    well_ssem,
    well_rsem,
    halo_ssem,
    halo_rsem,
    coef_ssem,
    coef_rsem,
    down_ssem,
    down_rsem,
    up_ssem,
    up_rsem,
):
    groups, n_gx, n_gy = dims
    tiles = n_gx * n_gy
    depth, width_x, width_y = field.shape
    slots = well_v.shape[1]
    own_wells = rate_v.shape[1]
    wells = tiles * own_wells
    me_l, me_x, me_y = lax.axis_index("layer"), lax.axis_index("gx"), lax.axis_index("gy")
    me = me_x * n_gy + me_y

    loads = [
        pltpu.make_async_copy(a, b, load_sem.at[i])
        for i, (a, b) in enumerate(
            [
                (pressure, field),
                (column_in, column_v),
                (well_in, well_v),
                (owner_in, owner_v),
                (index_in, index_v),
                (count_in, count_v),
                (rate_in, rate_v),
                (perm_x, kx),
                (perm_y, ky),
                (source, src),
                (robin, lower),
                (inverse, inv),
            ]
        )
    ]
    for load in loads:
        load.start()

    def peer(step):
        other = lax.rem(me + step, tiles)
        return {"gx": lax.div(other, n_gy), "gy": lax.rem(other, n_gy)}

    barrier = pltpu.get_barrier_semaphore()
    for step in range(1, tiles):
        pl.semaphore_signal(barrier, inc=1, device_id=peer(step), device_id_type=MESH)
    for step in range(1, groups):
        pl.semaphore_signal(
            barrier, inc=1, device_id={"layer": lax.rem(me_l + step, groups)}, device_id_type=MESH
        )

    for load in loads[1:7]:
        load.wait()
    live = lax.broadcasted_iota(jnp.int32, (slots, 1), 0) < count_v[...]
    column_row = column_v[...]
    column_col = as_column(column_row.astype(F32)).astype(jnp.int32)
    lane_x = lax.broadcasted_iota(jnp.int32, (slots, width_x), 1)
    in_x = (column_col >= lane_x * width_y) & (column_col < lane_x * width_y + width_y)
    x_of = jnp.sum(jnp.where(in_x, lane_x.astype(F32), 0.0), axis=1, keepdims=True).astype(jnp.int32)
    in_y = lax.broadcasted_iota(jnp.int32, (slots, width_y), 1) == column_col - x_of * width_y
    hot_x = jnp.where(in_x, 1.0, 0.0).astype(BF16)
    hot_x3 = jnp.concatenate([hot_x] * 3, axis=1)
    row_x = lax.broadcasted_iota(jnp.int32, (width_x, slots), 0)
    hot_xt = jnp.where(
        (column_row >= row_x * width_y) & (column_row < row_x * width_y + width_y), 1.0, 0.0
    ).astype(BF16)
    hot_xt3 = jnp.concatenate([hot_xt] * 3, axis=1)
    well_col = as_column(well_v[...].astype(F32)).astype(jnp.int32)
    well_id = owner_v[0] * own_wells + well_col
    member = jnp.where(
        (lax.broadcasted_iota(jnp.int32, (slots, wells), 1) == well_id) & live, 1.0, 0.0
    )
    index = index_v[...]
    rate_col = as_column(rate_v[...])
    rate_spot = (
        lax.broadcasted_iota(jnp.int32, (own_wells, wells), 1)
        == lax.broadcasted_iota(jnp.int32, (own_wells, wells), 0) + me * own_wells
    )
    rate_row = jnp.sum(jnp.where(rate_spot, rate_col, 0.0), axis=0, keepdims=True)
    layer_lane = lax.broadcasted_iota(jnp.int32, (slots, depth), 1)

    def gathered():
        at = jnp.zeros((slots, depth), F32)
        for l in range(depth):
            picked = jnp.dot(hot_x3, pieces(field[l]), preferred_element_type=F32)
            one = jnp.sum(jnp.where(in_y, picked, 0.0), axis=1, keepdims=True)
            at = jnp.where(layer_lane == l, one, at)
        return at

    def well_row(at):
        share = jnp.sum(index * at, axis=1, keepdims=True)
        return jnp.sum(share * member, axis=0, keepdims=True) + rate_row

    def well_copy(it, step):
        send, recv = ((well_send0, well_recv0), (well_send1, well_recv1))[it]
        return pltpu.make_async_remote_copy(
            src_ref=send,
            dst_ref=recv.at[step],
            send_sem=well_ssem.at[it, step],
            recv_sem=well_rsem.at[it, step],
            device_id=peer(step),
            device_id_type=MESH,
        )

    sides = (
        ("gx", me_x, -1, me_x > 0),
        ("gx", me_x, 1, me_x < n_gx - 1),
        ("gy", me_y, -1, me_y > 0),
        ("gy", me_y, 1, me_y < n_gy - 1),
    )

    def halo_copy(it, side):
        axis, mine, way, _ = sides[side]
        send, recv = (row_send, row_recv) if side < 2 else (col_send, col_recv)
        width = slice(0, 2 if it == 0 else 1)
        if side < 2:
            source_ref = send.at[it, side, width]
            target_ref = recv.at[it, 1 - side, width]
        else:
            source_ref = send.at[it, side - 2]
            target_ref = recv.at[it, 3 - side]
        return pltpu.make_async_remote_copy(
            src_ref=source_ref,
            dst_ref=target_ref,
            send_sem=halo_ssem.at[it, side],
            recv_sem=halo_rsem.at[it, side ^ 1],
            device_id={axis: mine + way},
            device_id_type=MESH,
        )

    def halo_landing(it, side):
        axis, mine, way, _ = sides[side]
        if side < 2:
            width = slice(0, 2 if it == 0 else 1)
            ref, other = row_recv.at[it, side, width], row_send.at[it, 1 - side, width]
        else:
            ref, other = col_recv.at[it, side - 2], col_send.at[it, 3 - side]
        return pltpu.make_async_remote_copy(
            src_ref=other,
            dst_ref=ref,
            send_sem=halo_ssem.at[it, side],
            recv_sem=halo_rsem.at[it, side],
            device_id={axis: mine + way},
            device_id_type=MESH,
        )

    lane128 = lax.broadcasted_iota(jnp.int32, (width_x, 128), 1)

    def packed_columns(arrays, lane):
        out = jnp.zeros((width_x, 128), F32)
        at = 0
        for ref in arrays:
            for l in range(depth):
                out = jnp.where(lane128 == at, ref[l, :, lane : lane + 1], out)
                at += 1
        return out

    def stage_halos(it):
        for l in range(depth):
            row_send[it, 0, 0, l : l + 1, :] = field[l, 0:1, :]
            row_send[it, 1, 0, l : l + 1, :] = field[l, width_x - 1 : width_x, :]
            if it == 0:
                row_send[it, 0, 1, l : l + 1, :] = kx[l, 0:1, :]
                row_send[it, 1, 1, l : l + 1, :] = kx[l, width_x - 1 : width_x, :]
        arrays = (field, ky) if it == 0 else (field,)
        col_send[it, 0] = packed_columns(arrays, 0)
        col_send[it, 1] = packed_columns(arrays, width_y - 1)
        for side in range(4):

            @pl.when(jnp.logical_not(sides[side][3]))
            def _():
                if side < 2:
                    row_recv[it, side] = jnp.zeros(row_recv.shape[2:], F32)
                else:
                    col_recv[it, side - 2] = jnp.zeros(col_recv.shape[2:], F32)

    def start_halos(it):
        for side in range(4):
            @pl.when(sides[side][3])
            def _():
                halo_copy(it, side).start()

    def wait_halos(it):
        for side in range(4):
            @pl.when(sides[side][3])
            def _():
                halo_landing(it, side).wait_recv()

    last_x = lax.broadcasted_iota(jnp.int32, (width_x, width_y), 0) == width_x - 1
    first_x = lax.broadcasted_iota(jnp.int32, (width_x, width_y), 0) == 0
    last_y = lax.broadcasted_iota(jnp.int32, (width_x, width_y), 1) == width_y - 1
    first_y = lax.broadcasted_iota(jnp.int32, (width_x, width_y), 1) == 0

    def next_x(value, row):
        return jnp.where(last_x, row, pltpu.roll(value, width_x - 1, 0))

    def next_y(value, col):
        return jnp.where(last_y, col, pltpu.roll(value, width_y - 1, 1))

    def face_coefficients():
        for l in range(depth):
            row = kx[l, 0:1, :]
            halo_mult_x[l : l + 1, :] = 0.5 * (row + row_recv[0, 0, 1, l : l + 1, :])
            mult = kx[l]
            kx[l] = 0.5 * (mult + next_x(mult, row_recv[0, 1, 1, l : l + 1, :]))
            mult = ky[l]
            ky[l] = 0.5 * (mult + next_y(mult, col_recv[0, 1, :, depth + l : depth + l + 1]))
        halo_mult_y[...] = 0.5 * (col_send[0, 0] + col_recv[0, 0])

    def lateral_sum(it):
        for l in range(depth):
            now = field[l]
            face_x, face_y = kx[l], ky[l]
            east = face_x * next_x(now, row_recv[it, 1, 0, l : l + 1, :])
            west_row = halo_mult_x[l : l + 1, :] * row_recv[it, 0, 0, l : l + 1, :]
            west = jnp.where(first_x, west_row, pltpu.roll(face_x * now, 1, 0))
            north = face_y * next_y(now, col_recv[it, 1, :, l : l + 1])
            south_col = halo_mult_y[:, depth + l : depth + l + 1] * col_recv[it, 0, :, l : l + 1]
            south = jnp.where(first_y, south_col, pltpu.roll(face_y * now, 1, 1))
            rhs[l] = src[l] + ((east + west) + (north + south))

    def layer_copy(ref, target, ssem, rsem, other):
        return pltpu.make_async_remote_copy(
            src_ref=ref,
            dst_ref=target,
            send_sem=ssem,
            recv_sem=rsem,
            device_id={"layer": other},
            device_id_type=MESH,
        )

    last = depth - 1
    coef_at = ((0, 0), (0, last), (last, 0))[: 1 if groups == 2 else 3]

    def coef_copy(which, sender, other):
        i, j = coef_at[which]
        return layer_copy(
            inv.at[i, j],
            coef_recv.at[sender, which],
            coef_ssem.at[other, which],
            coef_rsem.at[sender, which],
            other,
        )

    def coef_sent(which, sender, other):
        if which == 0:
            return other < sender
        if which == 1:
            return other < sender < groups - 1
        return 0 < sender < groups - 1

    def down_copy(it, sender, other):
        return layer_copy(
            down_send.at[it], down_recv.at[it, sender], down_ssem.at[it, other],
            down_rsem.at[it, sender], other,
        )

    def up_copy(it, sender, other):
        return layer_copy(
            up_send.at[it], up_recv.at[it, sender], up_ssem.at[it, other],
            up_rsem.at[it, sender], other,
        )

    def layer_sends(act, which):
        for g in range(groups):

            @pl.when(me_l == g)
            def _():
                for other in range(groups):
                    if other == g:
                        continue
                    if which == "coef":
                        for c in range(len(coef_at)):
                            if coef_sent(c, g, other):
                                getattr(coef_copy(c, g, other), act)()
                    else:
                        it = which
                        if g < groups - 1:
                            getattr(down_copy(it, g, other), act)()
                        if other < g:
                            getattr(up_copy(it, g, other), act)()

    def chunk_loop(body):
        def step(c, carry):
            body(pl.ds(pl.multiple_of(c * ROWS, ROWS), ROWS))
            return carry

        lax.fori_loop(0, width_x // ROWS, step, 0)

    def dot_layer(i, rows, terms):
        total = inv[i, 0, rows, :] * terms[0]
        for j in range(1, depth):
            total = total + inv[i, j, rows, :] * terms[j]
        return total

    def solve_faces(it):
        def body(rows):
            terms = [rhs[j, rows, :] for j in range(depth)]
            bottom = dot_layer(last, rows, terms)
            top = dot_layer(0, rows, terms)
            solved[last, rows, :] = bottom
            solved[0, rows, :] = top
            below = lower[rows, :]
            nothing = jnp.zeros_like(below)
            down_send[it, rows, :] = inv[last, 0, rows, :] * nothing + (
                (bottom + inv[last, last, rows, :] * below) - below
            )
            up_send[it, rows, :] = inv[0, last, rows, :] * nothing + top

        chunk_loop(body)

    def solve_rest():
        def body(rows):
            terms = [rhs[j, rows, :] for j in range(depth)]
            for i in range(1, depth - 1):
                solved[i, rows, :] = dot_layer(i, rows, terms)

        chunk_loop(body)

    def sweeps(it):
        for g in range(groups):

            @pl.when(me_l == g)
            def _():
                for k in range(groups):
                    if k == g:
                        continue
                    if k < groups - 1:
                        down_copy(it, k, k).wait_recv()
                    if k > g:
                        up_copy(it, k, k).wait_recv()
                    if it == 0:
                        for c in range(len(coef_at)):
                            if coef_sent(c, k, g):
                                coef_copy(c, k, k).wait_recv()

                def body(rows):
                    def coef(which, k):
                        i, j = coef_at[which]
                        return inv[i, j, rows, :] if k == g else coef_recv[k, which, rows, :]

                    above = [jnp.zeros((ROWS, width_y), F32)]
                    for k in range(groups - 1):
                        value = down_send[it, rows, :] if k == g else down_recv[it, k, rows, :]
                        if k > 0:
                            value = coef(2, k) * above[k] + value
                        above.append(value)
                    below = jnp.zeros((ROWS, width_y), F32)
                    for k in range(groups - 1, g, -1):
                        value = (up_recv[it, k, rows, :] + coef(0, k) * above[k]) - above[k]
                        if k < groups - 1:
                            value = coef(1, k) * below + value
                        below = value
                    upper[rows, :] = above[g]
                    lower[rows, :] = below

                chunk_loop(body)

    def update():
        def body(rows):
            above, below = upper[rows, :], lower[rows, :]
            for i in range(depth):
                field[i, rows, :] = (
                    solved[i, rows, :]
                    + inv[i, 0, rows, :] * above
                    + inv[i, last, rows, :] * below
                )

        chunk_loop(body)

    index_total = None
    for it in range(ITERS):
        if it == 0:
            loads[0].wait()
        at = gathered()
        if it == 0:
            index_row = jnp.sum(
                jnp.sum(index, axis=1, keepdims=True) * member, axis=0, keepdims=True
            )
            well_send0[...] = jnp.concatenate([well_row(at), index_row], axis=1)
            pl.semaphore_wait(barrier, tiles - 1 + groups - 1)
        else:
            well_send1[...] = well_row(at)
        for step in range(1, tiles):
            well_copy(it, step).start()
        if it == 0:
            loads[7].wait()
            loads[8].wait()
        stage_halos(it)
        start_halos(it)
        if it == 0:
            for load in loads[9:]:
                load.wait()
            layer_sends("start", "coef")
        wait_halos(it)
        if it == 0:
            face_coefficients()
        lateral_sum(it)
        total = (well_send0, well_send1)[it][...]
        for step in range(1, tiles):
            well_copy(it, step).wait_recv()
        for step in range(1, tiles):
            total = total + (well_recv0, well_recv1)[it][step]
        if it == 0:
            index_total = total[:, wells:] + 1.0
            total = total[:, :wells]
        bottom_hole = total / index_total
        hole = jnp.sum(member * bottom_hole, axis=1, keepdims=True)
        flow = jnp.where(live, index * (hole - at), 0.0)
        if it == ITERS - 1:
            flow_v[...] = flow
            flow_store = pltpu.make_async_copy(flow_v, flow_out, store_sem.at[0])
            flow_store.start()
        for l in range(depth):
            spread = jnp.where(in_y, flow[:, l : l + 1], 0.0)
            rhs[l] = rhs[l] + jnp.dot(hot_xt3, pieces(spread), preferred_element_type=F32)
        solve_faces(it)
        layer_sends("start", it)
        solve_rest()
        sweeps(it)
        update()
    field_store = pltpu.make_async_copy(field, field_out, store_sem.at[1])
    field_store.start()
    for it in range(ITERS):
        for step in range(1, tiles):
            well_copy(it, step).wait_send()
        for side in range(4):

            @pl.when(sides[side][3])
            def _():
                halo_copy(it, side).wait_send()

        layer_sends("wait_send", it)
    layer_sends("wait_send", "coef")
    flow_store.wait()
    field_store.wait()


def shards(
    pressure,
    source,
    perm_x,
    perm_y,
    line_inverse,
    robin_below,
    tile_count,
    perf_owner,
    perf_well,
    perf_column,
    perf_index,
    well_rate,
):
    depth, width_x, width_y = pressure.shape
    groups, n_gx, n_gy = (lax.axis_size(a) for a in ("layer", "gx", "gy"))
    tiles = n_gx * n_gy
    slots = perf_well.shape[1]
    own_wells = well_rate.shape[1]
    wells = tiles * own_wells
    sheet = (width_x, width_y)
    coefs = 1 if groups == 2 else 3
    anywhere = pl.BlockSpec(memory_space=pl.ANY)
    dma = pltpu.SemaphoreType.DMA
    i32 = jnp.int32
    call = pl.pallas_call(
        functools.partial(kernel, (groups, n_gx, n_gy)),
        out_shape=(
            jax.ShapeDtypeStruct(pressure.shape, F32),
            jax.ShapeDtypeStruct((slots, depth), F32),
        ),
        in_specs=[anywhere] * 12,
        out_specs=(anywhere, anywhere),
        scratch_shapes=[
            pltpu.VMEM(pressure.shape, F32),
            pltpu.VMEM(pressure.shape, F32),
            pltpu.VMEM(pressure.shape, F32),
            pltpu.VMEM(pressure.shape, F32),
            pltpu.VMEM((depth, depth) + sheet, F32),
            pltpu.VMEM(sheet, F32),
            pltpu.VMEM((1, 1), i32),
            pltpu.VMEM((1, slots, 1), i32),
            pltpu.VMEM((1, slots), i32),
            pltpu.VMEM((1, slots), i32),
            pltpu.VMEM((slots, depth), F32),
            pltpu.VMEM((1, own_wells), F32),
            pltpu.VMEM(sheet, F32),
            pltpu.VMEM(pressure.shape, F32),
            pltpu.VMEM(pressure.shape, F32),
            pltpu.VMEM((slots, depth), F32),
            pltpu.VMEM((depth, width_y), F32),
            pltpu.VMEM((width_x, 128), F32),
            pltpu.VMEM((1, 2 * wells), F32),
            pltpu.VMEM((tiles, 1, 2 * wells), F32),
            pltpu.VMEM((1, wells), F32),
            pltpu.VMEM((tiles, 1, wells), F32),
            pltpu.VMEM((ITERS, 2, 2, depth, width_y), F32),
            pltpu.VMEM((ITERS, 2, 2, depth, width_y), F32),
            pltpu.VMEM((ITERS, 2, width_x, 128), F32),
            pltpu.VMEM((ITERS, 2, width_x, 128), F32),
            pltpu.VMEM((groups, coefs) + sheet, F32),
            pltpu.VMEM((ITERS,) + sheet, F32),
            pltpu.VMEM((ITERS, groups) + sheet, F32),
            pltpu.VMEM((ITERS,) + sheet, F32),
            pltpu.VMEM((ITERS, groups) + sheet, F32),
            dma((12,)),
            dma((2,)),
            dma((ITERS, tiles)),
            dma((ITERS, tiles)),
            dma((ITERS, 4)),
            dma((ITERS, 4)),
            dma((groups, coefs)),
            dma((groups, coefs)),
            dma((ITERS, groups)),
            dma((ITERS, groups)),
            dma((ITERS, groups)),
            dma((ITERS, groups)),
        ],
        compiler_params=pltpu.CompilerParams(collective_id=0, has_side_effects=True),
        name="window",
    )
    field, flow = call(
        pressure,
        source,
        perm_x,
        perm_y,
        line_inverse[0],
        robin_below[0],
        tile_count,
        perf_owner,
        perf_well,
        perf_column,
        perf_index[0],
        well_rate,
    )
    return field, flow[None]


def solution(mesh):
    placed = (
        P("layer", "gx", "gy"),
        P("layer", "gx", "gy"),
        P("layer", "gx", "gy"),
        P("layer", "gx", "gy"),
        P("layer", None, None, "gx", "gy"),
        P("layer", "gx", "gy"),
        P("layer", ("gx", "gy")),
        P("layer", ("gx", "gy"), None),
        P("layer", ("gx", "gy")),
        P("layer", ("gx", "gy")),
        P("layer", ("gx", "gy"), None),
        P("layer", ("gx", "gy")),
    )
    return jax.shard_map(
        shards,
        mesh=mesh,
        in_specs=placed,
        out_specs=(P("layer", "gx", "gy"), P("layer", ("gx", "gy"), None)),
        check_vma=False,
    )
```

time: 162 us -> 32.4 us (0.20)
  starting transfers between devices: 62.7 us -> 0 us
  local copies, waits for them, and re-layouts: 45.4 us -> 5.99 us
  Pallas kernels: 0 us -> 24.8 us
  waiting for transfers between devices: 23.7 us -> 0 us
  other arithmetic: 22.6 us -> 0 us
  matrix products: 4.04 us -> 0 us
    ppermute x16 -> x0, starting transfers between devices: 36.5 us -> none  [the longest x6 21.2 us: extended(): before = lax.ppermute(last, axis, up)]
    all_to_all x5 -> x0, starting transfers between devices: 26.2 us -> none  [the longest x2 10.9 us: shards(): lax.all_to_all(outgoing, ('gx', 'gy'), split_axis=0, concat_axis=0, tiled...]
    pallas_call x0 -> x1, Pallas kernels: none -> 24.8 us  [shards(): call(pressure, source, perm_x, perm_y, line_inverse[0], robin_below[0], t...]
    reshape x10 -> x0, local copies, waits for them, and re-layouts: 15.7 us -> none  [the longest x2 11.7 us: shards(): well_term = jnp.zeros((layer_depth, columns), jnp.float32).at[:, column]....]
    ppermute x16 -> x0, waiting for transfers between devices: 13.6 us -> none  [the longest x4 13.6 us: passed_along(): lax.ppermute(value, axis, [(source, source + steps) for source in range(i...]
    all_to_all x5 -> x0, waiting for transfers between devices: 10.1 us -> none  [the longest x2 6.09 us: shards(): lax.all_to_all(outgoing, ('gx', 'gy'), split_axis=0, concat_axis=0, tiled...]
    scatter-add x2 -> x0, other arithmetic: 9.24 us -> none  [shards(): well_term = jnp.zeros((layer_depth, columns), jnp.float32).at[:, column]....]
    gather x2 -> x0, local copies, waits for them, and re-layouts: 7.93 us -> none  [shards(): at_slots = jnp.take(flat_field, column, axis=1).T]
  transfers between devices with their start and end apart: 21 -> 0, of which waited for: 8 -> 0; matrix products, arithmetic and copies ran while one was open for 31% -> 0% of each run, Pallas kernels for 0% -> 0%
where the time goes in v1:
time: 32.4 us; the launch traced here: 32.1 us
  Pallas kernels  24.8 us (77%)
  local copies, waits for them, and re-layouts  5.99 us (18%)
  between operations  1.29 us (4%)
    pallas_call x1, Pallas kernels, shards(): call(pressure, source, perm_x, perm_y, line_inverse[0], robin_below[0], t...  24.8 us
    unnamed x4, local copies, waits for them, and re-layouts  5.99 us

profile of v1, /device:TPU:0, one launch (start us, length us, event | category | flops | bytes accessed | tf_op | source)
XLA Modules:
  0.0 32.1 jit_solution(8288708496084802204)
XLA Ops:
  1.3 1.3 %copy.15.owner_in = s32[1,48,1]{2,1,0:T(8,128)} copy(s32[1,48,1]{1,2,0:T(1,128)} %param.19) | data formatting | bytes 384 | tf_op args[7]
  2.6 1.4 %copy.14 = f32[1,48,8]{2,1,0:T(8,128)} copy(f32[1,48,8]{1,2,0:T(8,128)} %param.22) | data formatting | bytes 3072 | tf_op args[10]
  4.0 24.8 %window.1 = (f32[8,64,256]{2,1,0:T(8,128)}, f32[48,8]{1,0:T(8,128)}) custom-call(f32[8,64,256]{2,1,0:T(8,128)} %pressure.1, f32[8,64,256]{2,1,0:T(8,128)} %source.1, f32[8,64,256]{2,1,0:T(8,128)} %perm_x.1, f32[8,64,256]{2,1,0:T(8,128)} %perm_y.1, f32[8,8,64,256]{3,2,1,0:T(8,128)} %bitcast.4, f32[64,256]{1,0:T(8,128)} %bitcast.6, s32[1,1]{1,0:T(1,128)S(6)} %copy.18.count_in, ...), custom_call_target="tpu_custom_call" | custom-call | tf_op jit(solution)/shard_map/window/pallas_call | solution.py:602
  28.8 1.4 %copy.16 = f32[1,48,8]{1,2,0:T(8,128)} copy(f32[1,48,8]{2,1,0:T(8,128)} %bitcast.7) | data formatting | bytes 3072
  30.2 1.9 %copy.19 = f32[8,64,256]{2,1,0:T(8,128)} copy(f32[8,64,256]{2,1,0:T(8,128)} %get-tuple-element.10) | data formatting | bytes 1048576

commit v2 on v1

--- a/solution.py
+++ b/solution.py
@@ -8,6 +8,7 @@
 from jax.sharding import PartitionSpec as P
 
 ITERS = 2
+LIMIT = 24 << 20
 MESH = pl.DeviceIdType.MESH
 F32 = jnp.float32
 BF16 = jnp.bfloat16
@@ -26,6 +27,23 @@
     n = row.shape[1]
     eye = lax.broadcasted_iota(jnp.int32, (n, n), 0) == lax.broadcasted_iota(jnp.int32, (n, n), 1)
     return jnp.sum(jnp.where(eye, jnp.broadcast_to(row, (n, n)), 0.0), axis=1, keepdims=True)
+
+
+def as_row(column):
+    n = column.shape[0]
+    eye = lax.broadcasted_iota(jnp.int32, (n, n), 0) == lax.broadcasted_iota(jnp.int32, (n, n), 1)
+    return jnp.sum(jnp.where(eye, jnp.broadcast_to(column, (n, n)), 0.0), axis=0, keepdims=True)
+
+
+def keep(field_in, flow_in, field_out, flow_out, sem):
+    copies = [
+        pltpu.make_async_copy(field_in, field_out, sem.at[0]),
+        pltpu.make_async_copy(flow_in, flow_out, sem.at[1]),
+    ]
+    for copy in copies:
+        copy.start()
+    for copy in copies:
+        copy.wait()
 
 
 def kernel(
@@ -148,18 +166,21 @@
     ).astype(BF16)
     hot_xt3 = jnp.concatenate([hot_xt] * 3, axis=1)
     well_col = as_column(well_v[...].astype(F32)).astype(jnp.int32)
-    well_id = owner_v[0] * own_wells + well_col
+    owner_col = as_column(owner_v[...].astype(F32)).astype(jnp.int32)
+    well_id = owner_col * own_wells + well_col
     member = jnp.where(
         (lax.broadcasted_iota(jnp.int32, (slots, wells), 1) == well_id) & live, 1.0, 0.0
     )
-    index = index_v[...]
+    layer_lane = lax.broadcasted_iota(jnp.int32, (slots, depth), 1)
+    index = jnp.zeros((slots, depth), F32)
+    for l in range(depth):
+        index = jnp.where(layer_lane == l, as_column(index_v[l : l + 1, :]), index)
     rate_col = as_column(rate_v[...])
     rate_spot = (
         lax.broadcasted_iota(jnp.int32, (own_wells, wells), 1)
         == lax.broadcasted_iota(jnp.int32, (own_wells, wells), 0) + me * own_wells
     )
     rate_row = jnp.sum(jnp.where(rate_spot, rate_col, 0.0), axis=0, keepdims=True)
-    layer_lane = lax.broadcasted_iota(jnp.int32, (slots, depth), 1)
 
     def gathered():
         at = jnp.zeros((slots, depth), F32)
@@ -490,7 +511,8 @@
         hole = jnp.sum(member * bottom_hole, axis=1, keepdims=True)
         flow = jnp.where(live, index * (hole - at), 0.0)
         if it == ITERS - 1:
-            flow_v[...] = flow
+            for l in range(depth):
+                flow_v[l : l + 1, :] = as_row(flow[:, l : l + 1])
             flow_store = pltpu.make_async_copy(flow_v, flow_out, store_sem.at[0])
             flow_store.start()
         for l in range(depth):
@@ -540,6 +562,7 @@
     wells = tiles * own_wells
     sheet = (width_x, width_y)
     coefs = 1 if groups == 2 else 3
+    HBM = pl.BlockSpec(memory_space=pltpu.HBM)
     anywhere = pl.BlockSpec(memory_space=pl.ANY)
     dma = pltpu.SemaphoreType.DMA
     i32 = jnp.int32
@@ -547,9 +570,9 @@
         functools.partial(kernel, (groups, n_gx, n_gy)),
         out_shape=(
             jax.ShapeDtypeStruct(pressure.shape, F32),
-            jax.ShapeDtypeStruct((slots, depth), F32),
+            jax.ShapeDtypeStruct((depth, slots), F32),
         ),
-        in_specs=[anywhere] * 12,
+        in_specs=[HBM] * 12,
         out_specs=(anywhere, anywhere),
         scratch_shapes=[
             pltpu.VMEM(pressure.shape, F32),
@@ -559,15 +582,15 @@
             pltpu.VMEM((depth, depth) + sheet, F32),
             pltpu.VMEM(sheet, F32),
             pltpu.VMEM((1, 1), i32),
-            pltpu.VMEM((1, slots, 1), i32),
             pltpu.VMEM((1, slots), i32),
             pltpu.VMEM((1, slots), i32),
-            pltpu.VMEM((slots, depth), F32),
+            pltpu.VMEM((1, slots), i32),
+            pltpu.VMEM((depth, slots), F32),
             pltpu.VMEM((1, own_wells), F32),
             pltpu.VMEM(sheet, F32),
             pltpu.VMEM(pressure.shape, F32),
             pltpu.VMEM(pressure.shape, F32),
-            pltpu.VMEM((slots, depth), F32),
+            pltpu.VMEM((depth, slots), F32),
             pltpu.VMEM((depth, width_y), F32),
             pltpu.VMEM((width_x, 128), F32),
             pltpu.VMEM((1, 2 * wells), F32),
@@ -596,10 +619,10 @@
             dma((ITERS, groups)),
             dma((ITERS, groups)),
         ],
-        compiler_params=pltpu.CompilerParams(collective_id=0, has_side_effects=True),
+        compiler_params=pltpu.CompilerParams(collective_id=0, has_side_effects=True, vmem_limit_bytes=LIMIT),
         name="window",
     )
-    field, flow = call(
+    operands = (
         pressure,
         source,
         perm_x,
@@ -607,13 +630,28 @@
         line_inverse[0],
         robin_below[0],
         tile_count,
-        perf_owner,
+        perf_owner[:, :, 0],
         perf_well,
         perf_column,
-        perf_index[0],
+        perf_index[0].T,
         well_rate,
     )
-    return field, flow[None]
+    field, flow = call(
+        *[x if x.size == 1 else pltpu.with_memory_space_constraint(x, pltpu.HBM) for x in operands]
+    )
+    field, flow = pl.pallas_call(
+        keep,
+        out_shape=(
+            jax.ShapeDtypeStruct(field.shape, F32),
+            jax.ShapeDtypeStruct(flow.shape, F32),
+        ),
+        in_specs=[anywhere] * 2,
+        out_specs=(HBM, HBM),
+        scratch_shapes=[dma((2,))],
+        compiler_params=pltpu.CompilerParams(vmem_limit_bytes=1 << 20),
+        name="keep",
+    )(field, flow)
+    return field, flow.T[None]
 
 
 def solution(mesh):

time: 32.4 us -> 26.5 us (0.82)
  local copies, waits for them, and re-layouts: 5.99 us -> 0 us
    unnamed x4 -> x0, local copies, waits for them, and re-layouts: 5.99 us -> none
    pallas_call x1 -> x2, Pallas kernels: 24.8 us -> 25.1 us  [the longest x1 24.2 us: shards(): call(*[x if x.size == 1 else pltpu.with_memory_space_constraint(x, pltpu....]
where the time goes in v2:
time: 26.5 us; the launch traced here: 26.3 us
  Pallas kernels  25.1 us (95%)
  between operations  1.29 us (5%)
    pallas_call x1, Pallas kernels, shards(): call(*[x if x.size == 1 else pltpu.with_memory_space_constraint(x, pltpu....  24.2 us
    pallas_call x1, Pallas kernels, shards(): pl.pallas_call(keep, out_shape=(jax.ShapeDtypeStruct(field.shape, F32), j...  0.81 us

profile of v2, /device:TPU:0, one launch (start us, length us, event | category | flops | bytes accessed | tf_op | source)
XLA Modules:
  0.0 26.3 jit_solution(11600355139128097513)
XLA Ops:
  1.3 24.2 %window.1 = (f32[8,64,256]{2,1,0:T(8,128)S(1)}, f32[8,48]{1,0:T(8,128)S(1)}) custom-call(f32[8,64,256]{2,1,0:T(8,128)} %pressure.1, f32[8,64,256]{2,1,0:T(8,128)} %source.1, f32[8,64,256]{2,1,0:T(8,128)} %perm_x.1, f32[8,64,256]{2,1,0:T(8,128)} %perm_y.1, f32[8,8,64,256]{3,2,1,0:T(8,128)} %bitcast.9, f32[64,256]{1,0:T(8,128)} %bitcast.10, ...), custom_call_target="tpu_custom_call" | custom-call | tf_op jit(solution)/shard_map/window/pallas_call | solution.py:639
  25.5 0.8 %keep.1 = (f32[8,64,256]{2,1,0:T(8,128)}, f32[8,48]{1,0:T(8,128)}) custom-call(f32[8,64,256]{2,1,0:T(8,128)S(1)} %get-tuple-element.6.field_in, f32[8,48]{1,0:T(8,128)S(1)} %get-tuple-element.7.flow_in), custom_call_target="tpu_custom_call" | custom-call | tf_op jit(solution)/shard_map/keep/pallas_call | solution.py:642

commit v3 on v2

--- a/solution.py
+++ b/solution.py
@@ -33,6 +33,21 @@
     n = column.shape[0]
     eye = lax.broadcasted_iota(jnp.int32, (n, n), 0) == lax.broadcasted_iota(jnp.int32, (n, n), 1)
     return jnp.sum(jnp.where(eye, jnp.broadcast_to(column, (n, n)), 0.0), axis=0, keepdims=True)
+
+
+def one_hots(column_row, width_x, width_y):
+    slots = column_row.shape[1]
+    column_col = as_column(column_row.astype(F32)).astype(jnp.int32)
+    lane_x = lax.broadcasted_iota(jnp.int32, (slots, width_x), 1)
+    in_x = (column_col >= lane_x * width_y) & (column_col < lane_x * width_y + width_y)
+    x_of = jnp.sum(jnp.where(in_x, lane_x.astype(F32), 0.0), axis=1, keepdims=True).astype(jnp.int32)
+    in_y = lax.broadcasted_iota(jnp.int32, (slots, width_y), 1) == column_col - x_of * width_y
+    hot_x = jnp.where(in_x, 1.0, 0.0).astype(BF16)
+    row_x = lax.broadcasted_iota(jnp.int32, (width_x, slots), 0)
+    hot_xt = jnp.where(
+        (column_row >= row_x * width_y) & (column_row < row_x * width_y + width_y), 1.0, 0.0
+    ).astype(BF16)
+    return in_y, jnp.concatenate([hot_x] * 3, axis=1), jnp.concatenate([hot_xt] * 3, axis=1)
 
 
 def keep(field_in, flow_in, field_out, flow_out, sem):
@@ -93,6 +108,10 @@
     down_recv,
     up_send,
     up_recv,
+    own_down,
+    spot_recv,
+    delta_send,
+    delta_recv,
     load_sem,
     store_sem,
     well_ssem,
@@ -105,6 +124,10 @@
     down_rsem,
     up_ssem,
     up_rsem,
+    spot_ssem,
+    spot_rsem,
+    delta_ssem,
+    delta_rsem,
 ):
     groups, n_gx, n_gy = dims
     tiles = n_gx * n_gy
@@ -152,19 +175,7 @@
     for load in loads[1:7]:
         load.wait()
     live = lax.broadcasted_iota(jnp.int32, (slots, 1), 0) < count_v[...]
-    column_row = column_v[...]
-    column_col = as_column(column_row.astype(F32)).astype(jnp.int32)
-    lane_x = lax.broadcasted_iota(jnp.int32, (slots, width_x), 1)
-    in_x = (column_col >= lane_x * width_y) & (column_col < lane_x * width_y + width_y)
-    x_of = jnp.sum(jnp.where(in_x, lane_x.astype(F32), 0.0), axis=1, keepdims=True).astype(jnp.int32)
-    in_y = lax.broadcasted_iota(jnp.int32, (slots, width_y), 1) == column_col - x_of * width_y
-    hot_x = jnp.where(in_x, 1.0, 0.0).astype(BF16)
-    hot_x3 = jnp.concatenate([hot_x] * 3, axis=1)
-    row_x = lax.broadcasted_iota(jnp.int32, (width_x, slots), 0)
-    hot_xt = jnp.where(
-        (column_row >= row_x * width_y) & (column_row < row_x * width_y + width_y), 1.0, 0.0
-    ).astype(BF16)
-    hot_xt3 = jnp.concatenate([hot_xt] * 3, axis=1)
+    in_y, hot_x3, hot_xt3 = one_hots(column_v[...], width_x, width_y)
     well_col = as_column(well_v[...].astype(F32)).astype(jnp.int32)
     owner_col = as_column(owner_v[...].astype(F32)).astype(jnp.int32)
     well_id = owner_col * own_wells + well_col
@@ -182,10 +193,10 @@
     )
     rate_row = jnp.sum(jnp.where(rate_spot, rate_col, 0.0), axis=0, keepdims=True)
 
-    def gathered():
+    def gathered(ref):
         at = jnp.zeros((slots, depth), F32)
         for l in range(depth):
-            picked = jnp.dot(hot_x3, pieces(field[l]), preferred_element_type=F32)
+            picked = jnp.dot(hot_x3, pieces(ref[l]), preferred_element_type=F32)
             one = jnp.sum(jnp.where(in_y, picked, 0.0), axis=1, keepdims=True)
             at = jnp.where(layer_lane == l, one, at)
         return at
@@ -294,33 +305,45 @@
     last_y = lax.broadcasted_iota(jnp.int32, (width_x, width_y), 1) == width_y - 1
     first_y = lax.broadcasted_iota(jnp.int32, (width_x, width_y), 1) == 0
 
-    def next_x(value, row):
-        return jnp.where(last_x, row, pltpu.roll(value, width_x - 1, 0))
-
-    def next_y(value, col):
-        return jnp.where(last_y, col, pltpu.roll(value, width_y - 1, 1))
-
     def face_coefficients():
         for l in range(depth):
-            row = kx[l, 0:1, :]
-            halo_mult_x[l : l + 1, :] = 0.5 * (row + row_recv[0, 0, 1, l : l + 1, :])
             mult = kx[l]
-            kx[l] = 0.5 * (mult + next_x(mult, row_recv[0, 1, 1, l : l + 1, :]))
+            kx[l] = 0.5 * (mult + pltpu.roll(mult, width_x - 1, 0))
             mult = ky[l]
-            ky[l] = 0.5 * (mult + next_y(mult, col_recv[0, 1, :, depth + l : depth + l + 1]))
+            ky[l] = 0.5 * (mult + pltpu.roll(mult, width_y - 1, 1))
+
+    def edge_coefficients():
+        for l in range(depth):
+            one = slice(l, l + 1)
+            halo_mult_x[one, :] = 0.5 * (row_send[0, 0, 1, one, :] + row_recv[0, 0, 1, one, :])
+            kx[l, width_x - 1 : width_x, :] = 0.5 * (
+                row_send[0, 1, 1, one, :] + row_recv[0, 1, 1, one, :]
+            )
+            lane = slice(depth + l, depth + l + 1)
+            ky[l, :, width_y - 1 : width_y] = 0.5 * (
+                col_send[0, 1, :, lane] + col_recv[0, 1, :, lane]
+            )
         halo_mult_y[...] = 0.5 * (col_send[0, 0] + col_recv[0, 0])
 
-    def lateral_sum(it):
+    def lateral_sum():
         for l in range(depth):
             now = field[l]
             face_x, face_y = kx[l], ky[l]
-            east = face_x * next_x(now, row_recv[it, 1, 0, l : l + 1, :])
-            west_row = halo_mult_x[l : l + 1, :] * row_recv[it, 0, 0, l : l + 1, :]
-            west = jnp.where(first_x, west_row, pltpu.roll(face_x * now, 1, 0))
-            north = face_y * next_y(now, col_recv[it, 1, :, l : l + 1])
-            south_col = halo_mult_y[:, depth + l : depth + l + 1] * col_recv[it, 0, :, l : l + 1]
-            south = jnp.where(first_y, south_col, pltpu.roll(face_y * now, 1, 1))
+            east = jnp.where(last_x, 0.0, face_x * pltpu.roll(now, width_x - 1, 0))
+            west = jnp.where(first_x, 0.0, pltpu.roll(face_x * now, 1, 0))
+            north = jnp.where(last_y, 0.0, face_y * pltpu.roll(now, width_y - 1, 1))
+            south = jnp.where(first_y, 0.0, pltpu.roll(face_y * now, 1, 1))
             rhs[l] = src[l] + ((east + west) + (north + south))
+
+    def lateral_edges(it):
+        end_x, end_y = slice(width_x - 1, width_x), slice(width_y - 1, width_y)
+        for l in range(depth):
+            one = slice(l, l + 1)
+            lane = slice(depth + l, depth + l + 1)
+            rhs[l, 0:1, :] += halo_mult_x[one, :] * row_recv[it, 0, 0, one, :]
+            rhs[l, end_x, :] += kx[l, end_x, :] * row_recv[it, 1, 0, one, :]
+            rhs[l, :, 0:1] += halo_mult_y[:, lane] * col_recv[it, 0, :, one]
+            rhs[l, :, end_y] += ky[l, :, end_y] * col_recv[it, 1, :, one]
 
     def layer_copy(ref, target, ssem, rsem, other):
         return pltpu.make_async_remote_copy(
@@ -351,6 +374,18 @@
         if which == 1:
             return other < sender < groups - 1
         return 0 < sender < groups - 1
+
+    def spot_copy(step):
+        return layer_copy(
+            column_v, spot_recv.at[step], spot_ssem.at[step], spot_rsem.at[step],
+            lax.rem(me_l + step, groups),
+        )
+
+    def delta_copy(it, step):
+        return layer_copy(
+            delta_send.at[it], delta_recv.at[it, step], delta_ssem.at[it, step],
+            delta_rsem.at[it, step], lax.rem(me_l + step, groups),
+        )
 
     def down_copy(it, sender, other):
         return layer_copy(
@@ -401,8 +436,6 @@
             terms = [rhs[j, rows, :] for j in range(depth)]
             bottom = dot_layer(last, rows, terms)
             top = dot_layer(0, rows, terms)
-            solved[last, rows, :] = bottom
-            solved[0, rows, :] = top
             below = lower[rows, :]
             nothing = jnp.zeros_like(below)
             down_send[it, rows, :] = inv[last, 0, rows, :] * nothing + (
@@ -412,11 +445,17 @@
 
         chunk_loop(body)
 
-    def solve_rest():
+    def solve_all():
         def body(rows):
             terms = [rhs[j, rows, :] for j in range(depth)]
-            for i in range(1, depth - 1):
-                solved[i, rows, :] = dot_layer(i, rows, terms)
+            for i in range(depth):
+                value = dot_layer(i, rows, terms)
+                solved[i, rows, :] = value
+                if i == last:
+                    below = lower[rows, :]
+                    own_down[rows, :] = inv[last, 0, rows, :] * jnp.zeros_like(below) + (
+                        (value + inv[last, last, rows, :] * below) - below
+                    )
 
         chunk_loop(body)
 
@@ -436,6 +475,16 @@
                         for c in range(len(coef_at)):
                             if coef_sent(c, k, g):
                                 coef_copy(c, k, k).wait_recv()
+                    step = (g - k) % groups
+                    delta_copy(it, step).wait_recv()
+                    other_y, _, other_xt3 = spots[step]
+                    for row, wanted, ref in ((0, k < groups - 1, down_recv), (1, k > g, up_recv)):
+                        if wanted:
+                            spread = as_column(delta_recv[it, step, row : row + 1, :])
+                            spread = pieces(jnp.where(other_y, spread, 0.0))
+                            ref[it, k] = ref[it, k] + jnp.dot(
+                                other_xt3, spread, preferred_element_type=F32
+                            )
 
                 def body(rows):
                     def coef(which, k):
@@ -444,7 +493,7 @@
 
                     above = [jnp.zeros((ROWS, width_y), F32)]
                     for k in range(groups - 1):
-                        value = down_send[it, rows, :] if k == g else down_recv[it, k, rows, :]
+                        value = own_down[rows, :] if k == g else down_recv[it, k, rows, :]
                         if k > 0:
                             value = coef(2, k) * above[k] + value
                         above.append(value)
@@ -472,33 +521,47 @@
         chunk_loop(body)
 
     index_total = None
+    spots = [None] * groups
     for it in range(ITERS):
         if it == 0:
             loads[0].wait()
-        at = gathered()
+        at = gathered(field)
         if it == 0:
             index_row = jnp.sum(
                 jnp.sum(index, axis=1, keepdims=True) * member, axis=0, keepdims=True
             )
             well_send0[...] = jnp.concatenate([well_row(at), index_row], axis=1)
+            loads[7].wait()
+            loads[8].wait()
+            stage_halos(it)
             pl.semaphore_wait(barrier, tiles - 1 + groups - 1)
         else:
             well_send1[...] = well_row(at)
         for step in range(1, tiles):
             well_copy(it, step).start()
-        if it == 0:
-            loads[7].wait()
-            loads[8].wait()
-        stage_halos(it)
+        if it > 0:
+            stage_halos(it)
         start_halos(it)
         if it == 0:
+            for step in range(1, groups):
+                spot_copy(step).start()
             for load in loads[9:]:
                 load.wait()
             layer_sends("start", "coef")
+        if it == 0:
+            face_coefficients()
+        lateral_sum()
         wait_halos(it)
         if it == 0:
-            face_coefficients()
-        lateral_sum(it)
+            edge_coefficients()
+        lateral_edges(it)
+        solve_faces(it)
+        layer_sends("start", it)
+        if it == 0:
+            for step in range(1, groups):
+                spot_copy(step).wait_recv()
+                spots[step] = one_hots(spot_recv[step], width_x, width_y)
+            face_last, face_first = gathered(inv.at[last]), gathered(inv.at[0])
         total = (well_send0, well_send1)[it][...]
         for step in range(1, tiles):
             well_copy(it, step).wait_recv()
@@ -510,6 +573,12 @@
         bottom_hole = total / index_total
         hole = jnp.sum(member * bottom_hole, axis=1, keepdims=True)
         flow = jnp.where(live, index * (hole - at), 0.0)
+        for row, face in enumerate((face_last, face_first)):
+            delta_send[it, row : row + 1, :] = as_row(
+                jnp.sum(face * flow, axis=1, keepdims=True)
+            )
+        for step in range(1, groups):
+            delta_copy(it, step).start()
         if it == ITERS - 1:
             for l in range(depth):
                 flow_v[l : l + 1, :] = as_row(flow[:, l : l + 1])
@@ -518,9 +587,7 @@
         for l in range(depth):
             spread = jnp.where(in_y, flow[:, l : l + 1], 0.0)
             rhs[l] = rhs[l] + jnp.dot(hot_xt3, pieces(spread), preferred_element_type=F32)
-        solve_faces(it)
-        layer_sends("start", it)
-        solve_rest()
+        solve_all()
         sweeps(it)
         update()
     field_store = pltpu.make_async_copy(field, field_out, store_sem.at[1])
@@ -535,6 +602,10 @@
                 halo_copy(it, side).wait_send()
 
         layer_sends("wait_send", it)
+        for step in range(1, groups):
+            delta_copy(it, step).wait_send()
+    for step in range(1, groups):
+        spot_copy(step).wait_send()
     layer_sends("wait_send", "coef")
     flow_store.wait()
     field_store.wait()
@@ -606,6 +677,10 @@
             pltpu.VMEM((ITERS, groups) + sheet, F32),
             pltpu.VMEM((ITERS,) + sheet, F32),
             pltpu.VMEM((ITERS, groups) + sheet, F32),
+            pltpu.VMEM(sheet, F32),
+            pltpu.VMEM((groups, 1, slots), i32),
+            pltpu.VMEM((ITERS, 2, slots), F32),
+            pltpu.VMEM((ITERS, groups, 2, slots), F32),
             dma((12,)),
             dma((2,)),
             dma((ITERS, tiles)),
@@ -616,6 +691,10 @@
             dma((groups, coefs)),
             dma((ITERS, groups)),
             dma((ITERS, groups)),
+            dma((ITERS, groups)),
+            dma((ITERS, groups)),
+            dma((groups,)),
+            dma((groups,)),
             dma((ITERS, groups)),
             dma((ITERS, groups)),
         ],

time: 26.5 us -> 24.9 us (0.940)
  Pallas kernels: 25.1 us -> 23.5 us
    pallas_call x1, Pallas kernels: 24.2 us -> 22.7 us  [shards(): call(*[x if x.size == 1 else pltpu.with_memory_space_constraint(x, pltpu....]
where the time goes in v3:
time: 24.9 us; the launch traced here: 24.8 us
  Pallas kernels  23.5 us (94%)
  between operations  1.29 us (5%)
    pallas_call x1, Pallas kernels, shards(): call(*[x if x.size == 1 else pltpu.with_memory_space_constraint(x, pltpu....  22.7 us
    pallas_call x1, Pallas kernels, shards(): pl.pallas_call(keep, out_shape=(jax.ShapeDtypeStruct(field.shape, F32), j...  0.81 us

profile of v3, /device:TPU:0, one launch (start us, length us, event | category | flops | bytes accessed | tf_op | source)
XLA Modules:
  0.0 24.8 jit_solution(9993732908615516502)
XLA Ops:
  1.3 22.7 %window.1 = (f32[8,64,256]{2,1,0:T(8,128)S(1)}, f32[8,48]{1,0:T(8,128)S(1)}) custom-call(f32[8,64,256]{2,1,0:T(8,128)} %pressure.1, f32[8,64,256]{2,1,0:T(8,128)} %source.1, f32[8,64,256]{2,1,0:T(8,128)} %perm_x.1, f32[8,64,256]{2,1,0:T(8,128)} %perm_y.1, f32[8,8,64,256]{3,2,1,0:T(8,128)} %bitcast.9, f32[64,256]{1,0:T(8,128)} %bitcast.10, ...), custom_call_target="tpu_custom_call" | custom-call | tf_op jit(solution)/shard_map/window/pallas_call | solution.py:718
  24.0 0.8 %keep.1 = (f32[8,64,256]{2,1,0:T(8,128)}, f32[8,48]{1,0:T(8,128)}) custom-call(f32[8,64,256]{2,1,0:T(8,128)S(1)} %get-tuple-element.6.field_in, f32[8,48]{1,0:T(8,128)S(1)} %get-tuple-element.7.flow_in), custom_call_target="tpu_custom_call" | custom-call | tf_op jit(solution)/shard_map/keep/pallas_call | solution.py:721
